TPU v7x, 256 devices: a whole 4x4x8 slice. The times are simulated.
256 devices in a mesh: row: 64 (over y, z, core), col: 4 (over x).
Axes of the slice: x: 4, y: 4, z: 8, core: 2. Of those that a mesh axis runs over, the one named last changes fastest.
Arguments:
- features: bfloat16 [65536, 256], P('row', 'col'), may hold values from -600 to 600
- tile_vals: bfloat16 [10240, 128, 128], P('row'), may hold values from -0.125 to 0.125
- tile_rows: int32 [64, 160], P('row'), may hold values from 0 to 7
- tile_srcs: int32 [64, 160], P('row'), may hold values from 0 to 135, as said below
- tile_count: int32 [64], P('row'), may hold values from 20 to 160, as said below
- needed: int32 [64, 64, 2], P('row'), may hold values from 0 to 7, as said below
- hop_noise: float32 [2, 65536, 256], P(None, 'row', 'col'), may hold values from -0.24 to 0.24
- enc_weight: bfloat16 [3, 256, 256], replicated, may hold values from -3.59375 to 3.59375
Outputs:
- encoded: bfloat16 [65536, 256], P('row', 'col')
Inputs may be any that keep to these rules, and one draw needn't show every extreme that they name: `tile_count`: some row index has exactly 160 live slots; slots at or beyond a row index's count are ignored. `tile_srcs`: A value s below 8 names the row index's own block s; otherwise s = 8 + o * 2 + c names entry c of needed for owner o, and o is never the row index itself. needed[d, o, :] are 2 distinct block indices among owner o's 8 blocks.
All inputs are finite; a program needn't handle non-finite values.
Results may differ from a plain program's by a relative error of at most 0.0053.
Values may be sent and summed in bfloat16 or wider, within the bound.
No kernel may reach another device: no remote copies, remote signals or barrier semaphores. Data moves between devices by JAX's collectives and lax.ppermute only.
A program may use at most 64 MiB of HBM per device.

v0:
```python
import jax
import jax.numpy as jnp
from jax import lax
from jax.sharding import PartitionSpec as P

BLK = 128
BPD = 8
TPD = 160
CAP = 2
HOPS = 2
epsilon = 1e-06


def shards(features, tile_vals, tile_rows, tile_srcs, tile_count, needed, hop_noise, enc_weight):
    row_count = lax.axis_size("row")
    row_index = lax.axis_index("row")
    col_index = lax.axis_index("col")
    local_rows, local_width = features.shape
    sources = tile_srcs[0]
    block_rows = tile_rows[0]
    live_count = tile_count[0]
    wanted = needed[0]
    tile_order = jnp.arange(TPD, dtype=jnp.int32)
    onehot = (
        (block_rows[:, None] == jnp.arange(BPD, dtype=jnp.int32)[None, :])
        & (tile_order < live_count)[:, None]
    ).astype(jnp.float32)

    def normalize(values):
        squares = lax.psum(jnp.sum(values * values, axis=1), "col")
        return (values / jnp.sqrt(squares + epsilon)[:, None]).astype(jnp.bfloat16)

    remote = jnp.maximum(sources - BPD, 0)
    slot_table = wanted.reshape(-1)
    looked_up = jnp.sum(
        jnp.where(
            remote[:, None] == jnp.arange(row_count * CAP, dtype=jnp.int32)[None, :],
            slot_table[None, :],
            0,
        ),
        axis=1,
    )
    global_block = jnp.where(
        sources < BPD, row_index * BPD + sources, remote // CAP * BPD + looked_up
    )
    current = normalize(features.astype(jnp.float32))
    layers = [current]
    for hop_index in range(HOPS):
        whole = lax.all_gather(current.reshape(BPD, BLK * local_width), "row", axis=0, tiled=True)
        products = jnp.einsum(
            "tij,tjf->tif",
            tile_vals,
            jnp.take(whole, global_block, axis=0).reshape(TPD, BLK, local_width),
            preferred_element_type=jnp.float32,
        )
        summed = jnp.einsum("tr,tif->rif", onehot, products, precision=lax.Precision.HIGHEST)
        current = normalize(summed.reshape(local_rows, local_width) + hop_noise[hop_index])
        layers.append(current)
    stacked = jnp.stack(layers)
    weight_slice = lax.dynamic_slice_in_dim(
        enc_weight, col_index * local_width, local_width, axis=1
    )
    terms = jnp.einsum("kri,kio->ro", stacked, weight_slice, preferred_element_type=jnp.float32)
    encoded = lax.psum_scatter(terms, "col", scatter_dimension=1, tiled=True)
    return encoded.astype(jnp.bfloat16)


def solution(mesh):
    in_specs = (
        P("row", "col"),
        P("row", None, None),
        P("row", None),
        P("row", None),
        P("row"),
        P("row", None, None),
        P(None, "row", "col"),
        P(),
    )
    out_specs = P("row", "col")
    return jax.shard_map(shards, mesh=mesh, in_specs=in_specs, out_specs=out_specs, check_vma=False)
```

profile of v0, /device:TPU:8, one launch (start us, length us, event | category | flops | bytes accessed | tf_op | source)
XLA Modules:
  0.0 299.7 jit_solution(14227140690207375910)
XLA Ops:
  6.5 1.0 fusion.9
  7.5 10.5 %psum.21 = f32[1024]{0:T(1024)S(1)} all-reduce(f32[1024]{0:T(1024)S(1)} %fusion.9), channel_id=1, replica_groups=mesh['row'=64,'col'=4] {'col'}, use_global_device_ids=true, to_apply=%region_1.2 | all-reduce | flops 1024 | bytes 8192 | tf_op jit(solution)/shard_map/psum | solution.py:30
  18.0 0.9 fusion.10
  19.2 0.9 reshape.66
  20.2 0.8 copy.14
  21.7 1.0 slice_bitcast_fusion.1
  22.7 0.8 copy.24
  23.5 0.5 iota_compare_fusion.2
  24.0 0.7 compare_reduce_fusion
  24.7 0.7 add_maximum_fusion
  25.6 77.1 %all-gather.3.cloned.1.call-done = bf16[512,8192]{1,0:T(8,128)(2,1)} async-done(((bf16[8,8192]{1,0:T(8,128)(2,1)}), bf16[512,8192]{1,0:T(8,128)(2,1)}) %all-gather.3.cloned.1.call-update) | async-done | bytes 8388624 | tf_op jit(solution)/shard_map/all_gather | solution.py:49
  102.7 9.0 %gather_fusion = bf16[160,8192]{1,0:T(8,128)(2,1)S(1)} fusion(bf16[512,8192]{1,0:T(8,128)(2,1)} %all-gather.3.cloned.1.call-done, s32[1024]{0:T(1024)S(1)} %pad_clamp_fusion), kind=kCustom, calls=%fused_computation.clone | custom fusion | bytes 5243520 | tf_op jit(solution)/shard_map/jit(_take)/gather | solution.py:53
  111.8 1.8 broadcast_select_fusion.1
  113.6 8.4 %reshape.67 = bf16[160,128,64]{2,1,0:T(8,128)(2,1)} reshape(bf16[160,8192]{1,0:T(8,128)(2,1)} %broadcast_select_fusion.1) | data formatting | bytes 5242880 | tf_op jit(solution)/shard_map/reshape | solution.py:53
  122.0 7.7 %convolution_bitcast_fusion.1 = f32[160,128,64]{1,2,0:T(8,128)S(1)} fusion(bf16[160,128,64]{2,1,0:T(8,128)(2,1)} %reshape.67, bf16[160,128,128]{2,1,0:T(8,128)(2,1)} %param.11), kind=kOutput, calls=%fused_computation.9 | convolution fusion | flops 335544320 | bytes 13107200 | tf_op jit(solution)/shard_map/tij,tjf->tif/dot_general | solution.py:50
  129.8 4.7 %fusion.14 = (f32[8,128]{1,0:T(8,128)S(1)}, f32[8,128,64]{1,0,2:T(8,128)S(1)}) fusion(f32[8,8,8,128]{3,2,1,0:T(8,128)S(1)} %copy-done.3, f32[160,128,64]{1,2,0:T(8,128)S(1)} %convolution_bitcast_fusion.1, s32[160]{0:T(256)S(1)} %bitcast.59, pred[160]{0:T(512)(128)(4,1)S(1)} %copy-done.8), kind=kOutput, calls=%fused_computation.25 | convolution fusion | flops 126027264 | bytes 5772064 | tf_op jit(solution)/shard_map/tr,tif->rif/dot_general | solution.py:56
  134.8 10.4 %psum.22 = f32[1024]{0:T(1024)S(1)} all-reduce(f32[1024]{0:T(1024)S(1)} %bitcast.55), channel_id=1, replica_groups=mesh['row'=64,'col'=4] {'col'}, use_global_device_ids=true, to_apply=%region_4.6 | all-reduce | flops 1024 | bytes 8192 | tf_op jit(solution)/shard_map/psum | solution.py:30
  145.2 0.7 divide_convert_fusion.2
  146.9 0.7 divide_convert_fusion.1
  147.6 0.3 reduce-scatter.2.cloned.1.call-start
  147.9 0.7 fusion.31
  148.6 0.8 copy.25
  149.4 76.1 %all-gather.5.cloned.1.call-done = bf16[512,8192]{1,0:T(8,128)(2,1)} async-done(((bf16[8,8192]{1,0:T(8,128)(2,1)}), bf16[512,8192]{1,0:T(8,128)(2,1)}) %all-gather.5.cloned.1.call-update) | async-done | bytes 8388624 | tf_op jit(solution)/shard_map/all_gather | solution.py:49
  225.4 9.0 %gather_fusion.1 = bf16[160,8192]{1,0:T(8,128)(2,1)S(1)} fusion(bf16[512,8192]{1,0:T(8,128)(2,1)} %all-gather.5.cloned.1.call-done, s32[1024]{0:T(1024)S(1)} %pad_clamp_fusion), kind=kCustom, calls=%fused_computation.1.clone | custom fusion | bytes 5243520 | tf_op jit(solution)/shard_map/jit(_take)/gather | solution.py:53
  234.5 1.8 broadcast_select_fusion
  236.3 8.4 %reshape.70 = bf16[160,128,64]{2,1,0:T(8,128)(2,1)} reshape(bf16[160,8192]{1,0:T(8,128)(2,1)} %broadcast_select_fusion) | data formatting | bytes 5242880 | tf_op jit(solution)/shard_map/reshape | solution.py:53
  244.7 7.7 %convolution_bitcast_fusion = f32[160,128,64]{1,2,0:T(8,128)S(1)} fusion(bf16[160,128,64]{2,1,0:T(8,128)(2,1)} %reshape.70, bf16[160,128,128]{2,1,0:T(8,128)(2,1)} %param.11), kind=kOutput, calls=%fused_computation.8 | convolution fusion | flops 335544320 | bytes 13107200 | tf_op jit(solution)/shard_map/tij,tjf->tif/dot_general | solution.py:50
  252.5 4.7 %fusion.12 = (f32[8,128]{1,0:T(8,128)S(1)}, f32[8,128,64]{1,0,2:T(8,128)S(1)}) fusion(f32[8,8,8,128]{3,2,1,0:T(8,128)S(1)} %copy-done.4, f32[160,128,64]{1,2,0:T(8,128)S(1)} %convolution_bitcast_fusion, s32[160]{0:T(256)S(1)} %bitcast.60, pred[160]{0:T(512)(128)(4,1)S(1)} %copy-done.9), kind=kOutput, calls=%fused_computation.22 | convolution fusion | flops 126027264 | bytes 5772064 | tf_op jit(solution)/shard_map/tr,tif->rif/dot_general | solution.py:56
  257.3 10.4 %psum.23 = f32[1024]{0:T(1024)S(1)} all-reduce(f32[1024]{0:T(1024)S(1)} %bitcast.56), channel_id=1, replica_groups=mesh['row'=64,'col'=4] {'col'}, use_global_device_ids=true, to_apply=%region_6.8 | all-reduce | flops 1024 | bytes 8192 | tf_op jit(solution)/shard_map/psum | solution.py:30
  267.8 1.3 convolution_bitcast_fusion.2
  269.1 22.4 %reduce-scatter.2.cloned.1.call-done = f32[1024,64]{0,1:T(8,128)} async-done(((f32[1024,256]{0,1:T(8,128)}), f32[1024,64]{0,1:T(8,128)}) %reduce-scatter.2.cloned.1.call-update) | async-done | bytes 262160 | tf_op jit(solution)/shard_map/reduce_scatter | solution.py:64
  291.5 1.6 convert_element_type.26
  (42 shorter events, 2.0 us)
Async XLA Ops:
  6.5 261.2 %copy-start = (bf16[3,256,256]{2,1,0:T(8,128)(2,1)S(1)}, bf16[3,256,256]{2,1,0:T(8,128)(2,1)}, u32[]{:S(2)}) copy-start(bf16[3,256,256]{2,1,0:T(8,128)(2,1)} %param.17) | copy-start | bytes 1179652
  6.5 96.2 %all-gather.3.cloned.1.call-start = ((), (), s32[]{:S(2)}) async-start(), calls=%async_computation.1 | async-start | bytes 8519680 | tf_op jit(solution)/shard_map/all_gather | solution.py:49
  20.1 205.3 %all-gather.5.cloned.1.call-start = ((), (), s32[]{:S(2)}) async-start(), calls=%async_computation.2 | async-start | bytes 8519680 | tf_op jit(solution)/shard_map/all_gather | solution.py:49
  122.0 7.7 %copy-start.3 = (f32[8,8,8,128]{3,2,1,0:T(8,128)S(1)}, f32[8,8,8,128]{3,2,1,0:T(8,128)}, u32[]{:S(2)}) copy-start(f32[8,8,8,128]{3,2,1,0:T(8,128)} %copy.24) | copy-start | bytes 786436
  122.0 7.7 %copy-start.7 = (s32[1,160]{1,0:T(1,128)S(1)}, s32[1,160]{1,0:T(1,128)}, u32[]{:S(2)}) copy-start(s32[1,160]{1,0:T(1,128)} %param.12) | copy-start | bytes 1924
  122.0 7.7 %copy-start.8 = (pred[160]{0:T(512)(128)(4,1)S(1)}, pred[160]{0:T(512)(128)(4,1)}, u32[]{:S(2)}) copy-start(pred[160]{0:T(512)(128)(4,1)} %iota_compare_fusion.2) | copy-start | bytes 484
  129.7 15.5 %copy-start.1 = (f32[2,1024,64]{1,2,0:T(8,128)S(1)}, f32[2,1024,64]{1,2,0:T(8,128)}, u32[]{:S(2)}) copy-start(f32[2,1024,64]{1,2,0:T(8,128)} %param.16) | copy-start | bytes 1572868
  129.8 18.2 %copy-start.2 = (bf16[1024,64]{0,1:T(8,128)(2,1)S(1)}, bf16[1024,64]{0,1:T(8,128)(2,1)}, u32[]{:S(2)}) copy-start(bf16[1024,64]{0,1:T(8,128)(2,1)} %param.10) | copy-start | bytes 393220
  147.6 143.9 %reduce-scatter.2.cloned.1.call-start = ((), (), s32[]{:S(2)}) async-start(), calls=%async_computation.3 | async-start | bytes 1310720 | tf_op jit(solution)/shard_map/reduce_scatter | solution.py:64
  244.7 7.7 %copy-start.4 = (f32[8,8,8,128]{3,2,1,0:T(8,128)S(1)}, f32[8,8,8,128]{3,2,1,0:T(8,128)}, u32[]{:S(2)}) copy-start(f32[8,8,8,128]{3,2,1,0:T(8,128)} %copy.25) | copy-start | bytes 786436
  244.7 7.7 %copy-start.9 = (pred[160]{0:T(512)(128)(4,1)S(1)}, pred[160]{0:T(512)(128)(4,1)}, u32[]{:S(2)}) copy-start(pred[160]{0:T(512)(128)(4,1)} %iota_compare_fusion.2) | copy-start | bytes 484
  252.4 15.3 %copy-start.5 = (bf16[1,1024,64]{1,2,0:T(8,128)(2,1)S(1)}, bf16[1,1024,64]{1,2,0:T(8,128)(2,1)}, u32[]{:S(2)}) copy-start(bf16[1,1024,64]{1,2,0:T(8,128)(2,1)} %fusion.31) | copy-start | bytes 393220
  252.4 15.3 %copy-start.6 = (bf16[1,1024,64]{1,2,0:T(8,128)(2,1)S(1)}, bf16[1,1024,64]{1,2,0:T(8,128)(2,1)}, u32[]{:S(2)}) copy-start(bf16[1,1024,64]{1,2,0:T(8,128)(2,1)} %get-tuple-element.8) | copy-start | bytes 393220
Sparse Core Ops, SparseCore 0:
  20.2 82.4 all-gather.2
  147.8 77.6 all-gather.4
  269.3 22.2 reduce-scatter.1
where the time goes:
time: 300 us
  waiting for transfers between devices  176 us (59%)
  local copies, waits for them, and re-layouts  40.7 us (14%)
  blocking collectives  31.4 us (10%)
  matrix products  26.2 us (9%)
  between operations  14 us (5%)
  other arithmetic  11.5 us (4%)
    all_gather x2, waiting for transfers between devices, shards(): lax.all_gather(current.reshape(BPD, BLK * local_width), 'row', axis=0, ti...  153 us
    psum x3, blocking collectives, normalize(): squares = lax.psum(jnp.sum(values * values, axis=1), 'col')  31.4 us
    reduce_scatter x1, waiting for transfers between devices, shards(): encoded = lax.psum_scatter(terms, 'col', scatter_dimension=1, tiled=True)  22.4 us
    gather x2, local copies, waits for them, and re-layouts, shards(): jnp.take(whole, global_block, axis=0).reshape(TPD, BLK, local_width)  18.1 us
    reshape x2, local copies, waits for them, and re-layouts, shards(): jnp.take(whole, global_block, axis=0).reshape(TPD, BLK, local_width)  16.8 us
    dot_general x2, matrix products, shards(): jnp.einsum('tij,tjf->tif', tile_vals, jnp.take(whole, global_block, axis=...  15.4 us
    dot_general x2, matrix products, shards(): jnp.einsum('tr,tif->rif', onehot, products, precision=lax.Precision.HIGHEST)  9.47 us
  transfers between devices with their start and end apart: 3, of which 3 were waited for; matrix products, arithmetic and copies ran while one was open for 2% of the time, Pallas kernels for 0%

commit v1 on v0

--- a/solution.py
+++ b/solution.py
@@ -27,7 +27,7 @@
     ).astype(jnp.float32)
 
     def normalize(values):
-        squares = lax.psum(jnp.sum(values * values, axis=1), "col")
+        squares = jnp.sum(lax.all_gather(jnp.sum(values * values, axis=1), "col"), axis=0)
         return (values / jnp.sqrt(squares + epsilon)[:, None]).astype(jnp.bfloat16)
 
     remote = jnp.maximum(sources - BPD, 0)

time: 300 us -> 311 us (1.037)
  blocking collectives: 31.4 us -> 37 us
  waiting for transfers between devices: 176 us -> 180 us
    all_gather x0 -> x3, blocking collectives: none -> 37 us  [normalize(): lax.all_gather(jnp.sum(values * values, axis=1), 'col')]
    psum x3 -> x0, blocking collectives: 31.4 us -> none  [normalize(): squares = lax.psum(jnp.sum(values * values, axis=1), 'col')]
where the time goes in v1:
time: 311 us; the launch traced here: 310 us
  waiting for transfers between devices  180 us (58%)
  local copies, waits for them, and re-layouts  40.7 us (13%)
  blocking collectives  37 us (12%)
  matrix products  26.2 us (8%)
  between operations  14 us (5%)
  other arithmetic  11.5 us (4%)
    all_gather x2, waiting for transfers between devices, shards(): lax.all_gather(current.reshape(BPD, BLK * local_width), 'row', axis=0, ti...  156 us
    all_gather x3, blocking collectives, normalize(): lax.all_gather(jnp.sum(values * values, axis=1), 'col')  37 us
    reduce_scatter x1, waiting for transfers between devices, shards(): encoded = lax.psum_scatter(terms, 'col', scatter_dimension=1, tiled=True)  23.9 us
    gather x2, local copies, waits for them, and re-layouts, shards(): jnp.take(whole, global_block, axis=0).reshape(TPD, BLK, local_width)  18.1 us
    reshape x2, local copies, waits for them, and re-layouts, shards(): jnp.take(whole, global_block, axis=0).reshape(TPD, BLK, local_width)  16.8 us
    dot_general x2, matrix products, shards(): jnp.einsum('tij,tjf->tif', tile_vals, jnp.take(whole, global_block, axis=...  15.4 us
    dot_general x2, matrix products, shards(): jnp.einsum('tr,tif->rif', onehot, products, precision=lax.Precision.HIGHEST)  9.47 us
  transfers between devices with their start and end apart: 3, of which 3 were waited for; matrix products, arithmetic and copies ran while one was open for 2% of the time, Pallas kernels for 0%

profile of v1, /device:TPU:8, one launch (start us, length us, event | category | flops | bytes accessed | tf_op | source)
XLA Modules:
  0.0 310.0 jit_solution(4673200169003570598)
XLA Ops:
  6.5 1.0 fusion.9
  7.5 12.4 %all-gather = f32[4096]{0:T(1024)S(1)} all-gather(f32[1024]{0:T(1024)S(1)} %fusion.9), channel_id=2, replica_groups=mesh['row'=64,'col'=4] {'col'}, dimensions={0}, use_global_device_ids=true | all-gather | bytes 20480 | tf_op jit(solution)/shard_map/all_gather | solution.py:30
  19.9 0.9 fusion.10
  21.1 0.9 reshape.86
  22.1 0.8 copy.22
  23.6 1.0 slice_bitcast_fusion.1
  24.6 0.8 copy.32
  25.4 0.5 iota_compare_fusion.2
  25.9 0.7 compare_reduce_fusion
  26.6 0.7 add_maximum_fusion
  27.5 78.7 %all-gather.6.cloned.1.call-done = bf16[512,8192]{1,0:T(8,128)(2,1)} async-done(((bf16[8,8192]{1,0:T(8,128)(2,1)}), bf16[512,8192]{1,0:T(8,128)(2,1)}) %all-gather.6.cloned.1.call-update) | async-done | bytes 8388624 | tf_op jit(solution)/shard_map/all_gather | solution.py:49
  106.2 9.0 %gather_fusion = bf16[160,8192]{1,0:T(8,128)(2,1)S(1)} fusion(bf16[512,8192]{1,0:T(8,128)(2,1)} %all-gather.6.cloned.1.call-done, s32[1024]{0:T(1024)S(1)} %pad_clamp_fusion), kind=kCustom, calls=%fused_computation.clone | custom fusion | bytes 5243520 | tf_op jit(solution)/shard_map/jit(_take)/gather | solution.py:53
  115.2 1.8 broadcast_select_fusion.1
  117.1 8.4 %reshape.87 = bf16[160,128,64]{2,1,0:T(8,128)(2,1)} reshape(bf16[160,8192]{1,0:T(8,128)(2,1)} %broadcast_select_fusion.1) | data formatting | bytes 5242880 | tf_op jit(solution)/shard_map/reshape | solution.py:53
  125.5 7.7 %convolution_bitcast_fusion.1 = f32[160,128,64]{1,2,0:T(8,128)S(1)} fusion(bf16[160,128,64]{2,1,0:T(8,128)(2,1)} %reshape.87, bf16[160,128,128]{2,1,0:T(8,128)(2,1)} %param.11), kind=kOutput, calls=%fused_computation.9 | convolution fusion | flops 335544320 | bytes 13107200 | tf_op jit(solution)/shard_map/tij,tjf->tif/dot_general | solution.py:50
  133.2 4.7 %fusion.14 = (f32[8,128]{1,0:T(8,128)S(1)}, f32[8,128,64]{1,0,2:T(8,128)S(1)}) fusion(f32[8,8,8,128]{3,2,1,0:T(8,128)S(1)} %copy-done.3, f32[160,128,64]{1,2,0:T(8,128)S(1)} %convolution_bitcast_fusion.1, s32[160]{0:T(256)S(1)} %bitcast.59, pred[160]{0:T(512)(128)(4,1)S(1)} %copy-done.8), kind=kOutput, calls=%fused_computation.25 | convolution fusion | flops 126027264 | bytes 5772064 | tf_op jit(solution)/shard_map/tr,tif->rif/dot_general | solution.py:56
  138.2 12.3 %all-gather.1 = f32[4,1,1024]{2,1,0:T(1,128)S(1)} all-gather(f32[1,1,1024]{2,1,0:T(1,128)S(1)} %bitcast.55), channel_id=1, replica_groups=mesh['row'=64,'col'=4] {'col'}, dimensions={0}, use_global_device_ids=true | all-gather | bytes 20480 | tf_op jit(solution)/shard_map/all_gather | solution.py:30
  150.6 0.7 divide_convert_fusion.2
  152.3 0.7 divide_convert_fusion.1
  153.0 0.3 reduce-scatter.2.cloned.1.call-start
  153.3 0.7 fusion.31
  154.0 0.8 copy.33
  154.7 77.6 %all-gather.8.cloned.1.call-done = bf16[512,8192]{1,0:T(8,128)(2,1)} async-done(((bf16[8,8192]{1,0:T(8,128)(2,1)}), bf16[512,8192]{1,0:T(8,128)(2,1)}) %all-gather.8.cloned.1.call-update) | async-done | bytes 8388624 | tf_op jit(solution)/shard_map/all_gather | solution.py:49
  232.4 9.0 %gather_fusion.1 = bf16[160,8192]{1,0:T(8,128)(2,1)S(1)} fusion(bf16[512,8192]{1,0:T(8,128)(2,1)} %all-gather.8.cloned.1.call-done, s32[1024]{0:T(1024)S(1)} %pad_clamp_fusion), kind=kCustom, calls=%fused_computation.1.clone | custom fusion | bytes 5243520 | tf_op jit(solution)/shard_map/jit(_take)/gather | solution.py:53
  241.4 1.8 broadcast_select_fusion
  243.2 8.4 %reshape.90 = bf16[160,128,64]{2,1,0:T(8,128)(2,1)} reshape(bf16[160,8192]{1,0:T(8,128)(2,1)} %broadcast_select_fusion) | data formatting | bytes 5242880 | tf_op jit(solution)/shard_map/reshape | solution.py:53
  251.6 7.7 %convolution_bitcast_fusion = f32[160,128,64]{1,2,0:T(8,128)S(1)} fusion(bf16[160,128,64]{2,1,0:T(8,128)(2,1)} %reshape.90, bf16[160,128,128]{2,1,0:T(8,128)(2,1)} %param.11), kind=kOutput, calls=%fused_computation.8 | convolution fusion | flops 335544320 | bytes 13107200 | tf_op jit(solution)/shard_map/tij,tjf->tif/dot_general | solution.py:50
  259.4 4.7 %fusion.12 = (f32[8,128]{1,0:T(8,128)S(1)}, f32[8,128,64]{1,0,2:T(8,128)S(1)}) fusion(f32[8,8,8,128]{3,2,1,0:T(8,128)S(1)} %copy-done.4, f32[160,128,64]{1,2,0:T(8,128)S(1)} %convolution_bitcast_fusion, s32[160]{0:T(256)S(1)} %bitcast.60, pred[160]{0:T(512)(128)(4,1)S(1)} %copy-done.9), kind=kOutput, calls=%fused_computation.22 | convolution fusion | flops 126027264 | bytes 5772064 | tf_op jit(solution)/shard_map/tr,tif->rif/dot_general | solution.py:56
  264.2 12.3 %all-gather.2 = f32[4,1,1024]{2,1,0:T(1,128)S(1)} all-gather(f32[1,1,1024]{2,1,0:T(1,128)S(1)} %bitcast.56), channel_id=1, replica_groups=mesh['row'=64,'col'=4] {'col'}, dimensions={0}, use_global_device_ids=true | all-gather | bytes 20480 | tf_op jit(solution)/shard_map/all_gather | solution.py:30
  276.6 1.3 convolution_bitcast_fusion.2
  278.0 23.9 %reduce-scatter.2.cloned.1.call-done = f32[1024,64]{0,1:T(8,128)} async-done(((f32[1024,256]{0,1:T(8,128)}), f32[1024,64]{0,1:T(8,128)}) %reduce-scatter.2.cloned.1.call-update) | async-done | bytes 262160 | tf_op jit(solution)/shard_map/reduce_scatter | solution.py:64
  301.8 1.6 convert_element_type.26
  (46 shorter events, 2.0 us)
Async XLA Ops:
  6.5 270.0 %copy-start = (bf16[3,256,256]{2,1,0:T(8,128)(2,1)S(1)}, bf16[3,256,256]{2,1,0:T(8,128)(2,1)}, u32[]{:S(2)}) copy-start(bf16[3,256,256]{2,1,0:T(8,128)(2,1)} %param.17) | copy-start | bytes 1179652
  6.5 99.7 %all-gather.6.cloned.1.call-start = ((), (), s32[]{:S(2)}) async-start(), calls=%async_computation.1 | async-start | bytes 8519680 | tf_op jit(solution)/shard_map/all_gather | solution.py:49
  22.0 210.3 %all-gather.8.cloned.1.call-start = ((), (), s32[]{:S(2)}) async-start(), calls=%async_computation.2 | async-start | bytes 8519680 | tf_op jit(solution)/shard_map/all_gather | solution.py:49
  125.5 7.7 %copy-start.3 = (f32[8,8,8,128]{3,2,1,0:T(8,128)S(1)}, f32[8,8,8,128]{3,2,1,0:T(8,128)}, u32[]{:S(2)}) copy-start(f32[8,8,8,128]{3,2,1,0:T(8,128)} %copy.32) | copy-start | bytes 786436
  125.5 7.7 %copy-start.7 = (s32[1,160]{1,0:T(1,128)S(1)}, s32[1,160]{1,0:T(1,128)}, u32[]{:S(2)}) copy-start(s32[1,160]{1,0:T(1,128)} %param.12) | copy-start | bytes 1924
  125.5 7.7 %copy-start.8 = (pred[160]{0:T(512)(128)(4,1)S(1)}, pred[160]{0:T(512)(128)(4,1)}, u32[]{:S(2)}) copy-start(pred[160]{0:T(512)(128)(4,1)} %iota_compare_fusion.2) | copy-start | bytes 484
  133.2 17.4 %copy-start.1 = (f32[2,1024,64]{1,2,0:T(8,128)S(1)}, f32[2,1024,64]{1,2,0:T(8,128)}, u32[]{:S(2)}) copy-start(f32[2,1024,64]{1,2,0:T(8,128)} %param.16) | copy-start | bytes 1572868
  133.2 20.1 %copy-start.2 = (bf16[1024,64]{0,1:T(8,128)(2,1)S(1)}, bf16[1024,64]{0,1:T(8,128)(2,1)}, u32[]{:S(2)}) copy-start(bf16[1024,64]{0,1:T(8,128)(2,1)} %param.10) | copy-start | bytes 393220
  153.0 148.8 %reduce-scatter.2.cloned.1.call-start = ((), (), s32[]{:S(2)}) async-start(), calls=%async_computation.3 | async-start | bytes 1310720 | tf_op jit(solution)/shard_map/reduce_scatter | solution.py:64
  251.6 7.7 %copy-start.4 = (f32[8,8,8,128]{3,2,1,0:T(8,128)S(1)}, f32[8,8,8,128]{3,2,1,0:T(8,128)}, u32[]{:S(2)}) copy-start(f32[8,8,8,128]{3,2,1,0:T(8,128)} %copy.33) | copy-start | bytes 786436
  251.6 7.7 %copy-start.9 = (pred[160]{0:T(512)(128)(4,1)S(1)}, pred[160]{0:T(512)(128)(4,1)}, u32[]{:S(2)}) copy-start(pred[160]{0:T(512)(128)(4,1)} %iota_compare_fusion.2) | copy-start | bytes 484
  259.3 17.2 %copy-start.5 = (bf16[1,1024,64]{1,2,0:T(8,128)(2,1)S(1)}, bf16[1,1024,64]{1,2,0:T(8,128)(2,1)}, u32[]{:S(2)}) copy-start(bf16[1,1024,64]{1,2,0:T(8,128)(2,1)} %fusion.31) | copy-start | bytes 393220
  259.4 17.2 %copy-start.6 = (bf16[1,1024,64]{1,2,0:T(8,128)(2,1)S(1)}, bf16[1,1024,64]{1,2,0:T(8,128)(2,1)}, u32[]{:S(2)}) copy-start(bf16[1,1024,64]{1,2,0:T(8,128)(2,1)} %get-tuple-element.8) | copy-start | bytes 393220
Sparse Core Ops, SparseCore 0:
  22.1 84.0 all-gather.5
  153.1 79.1 all-gather.7
  278.1 23.6 reduce-scatter.1
